TPU v7x, 128 devices: a whole 4x4x4 slice. The times are simulated.
128 devices in a mesh: ctx: 8 (over x, core), tp: 16 (over z, y).
Axes of the slice: x: 4, y: 4, z: 4, core: 2. Of those that a mesh axis runs over, the one named last changes fastest.
Arguments:
- out_grad: bfloat16 [8192, 4096], P('ctx', 'tp'), may hold values from -6 to 6
- pre_act: bfloat16 [8192, 4096], P('ctx', 'tp'), may hold values from -6 to 6
- normed: bfloat16 [8192, 12800], P('ctx', 'tp'), may hold values from -5 to 5
- inverse_std: float32 [8192], P('ctx'), may hold values from 0.5 to 2
- w_up: bfloat16 [4096, 12800], P(None, 'tp')
- w_down: bfloat16 [4096, 4096], P(None, 'tp'), may hold values from -0.09375 to 0.09375
- ln_gain: float32 [12800], P('tp'), may hold values from 0.25 to 1.75
- owner_map: int32 [8, 4], P('ctx'), may hold values from 0 to 15, as said below
Outputs:
- grad_w2: float32 [4096, 4096], P('ctx', 'tp')
- grad_w1: float32 [4096, 12800], P('ctx', 'tp')
- grad_b1: float32 [4096], P('tp')
- grad_b2: float32 [4096], P('tp')
- ln_grads: float32 [2, 12800], P(None, 'tp')
- vit_grad: bfloat16 [32768, 12800], P(('ctx', 'tp'))
Inputs may be any that keep to these rules, and one draw needn't show every extreme that they name: `owner_map`: within each context shard, every encoder rank owns at most 1 of the 4 images, and some rank owns exactly 1.
All inputs are finite; a program needn't handle non-finite values.
Results may differ from a plain program's by a relative error of at most 0.007.
Values may be sent and summed in bfloat16 or wider, within the bound.
A program may use at most 192 MiB of HBM per device.

v0:
```python
import math
import jax
import jax.numpy as jnp
from jax import lax
from jax.sharding import PartitionSpec as P


def gelu_parts(linear):
    normal_cdf = 0.5 * (1.0 + jax.scipy.special.erf(linear * 2.0 ** (-0.5)))
    density = jnp.exp(-0.5 * linear * linear) * (2.0 * math.pi) ** (-0.5)
    return (linear * normal_cdf, normal_cdf + linear * density)


def slot_numbers(owners, capacity):
    position = jnp.arange(owners.shape[0])
    earlier = (owners[None, :] == owners[:, None]) & (position[None, :] < position[:, None])
    return owners * capacity + jnp.sum(earlier.astype(jnp.int32), axis=1)


def row_product(left, right):
    return lax.dot_general(
        left, right, (((0,), (0,)), ((), ())), preferred_element_type=jnp.float32
    )


def per_device(out_grad, pre_act, normed, inverse_std, w_up, w_down, ln_gain, owner_map):
    ctx_count = lax.axis_size("ctx")
    tp_count = lax.axis_size("tp")
    row_count = out_grad.shape[0]
    grad_scale = float(row_count * ctx_count) ** (-0.5)
    gelu_value, gelu_slope = gelu_parts(pre_act.astype(jnp.float32))
    hidden = gelu_value.astype(jnp.bfloat16)
    full_grad = lax.all_gather(out_grad, "tp", axis=1, tiled=True)
    back_hidden = jnp.dot(full_grad, w_down, preferred_element_type=jnp.float32)
    back_part = (back_hidden * gelu_slope).astype(jnp.bfloat16)
    columns = full_grad
    grad_w2 = (
        lax.psum_scatter(row_product(columns, hidden), "ctx", scatter_dimension=0, tiled=True)
        * grad_scale
    )
    bias_down, bias_up = lax.psum(
        (
            jnp.sum(out_grad.astype(jnp.float32), axis=0),
            jnp.sum(back_part.astype(jnp.float32), axis=0),
        ),
        "ctx",
    )
    back_linear = lax.all_gather(back_part, "tp", axis=1, tiled=True)
    columns = back_linear
    grad_w1 = (
        lax.psum_scatter(row_product(columns, normed), "ctx", scatter_dimension=0, tiled=True)
        * grad_scale
    )
    norm_grad = jnp.dot(back_linear, w_up, preferred_element_type=jnp.float32)
    features = normed.astype(jnp.float32)
    gained = ln_gain[None, :] * norm_grad
    sum_first, sum_second = lax.psum(
        (jnp.sum(gained, axis=-1), jnp.sum(gained * features, axis=-1)), "tp"
    )
    full_width = float(normed.shape[1] * tp_count)
    mean_first = sum_first / full_width
    mean_second = sum_second / full_width
    visual = (
        inverse_std[:, None] * (gained - mean_first[:, None] - features * mean_second[:, None])
    ).astype(jnp.bfloat16)
    gain_sum, bias_sum = lax.psum(
        (jnp.sum(norm_grad * features, axis=0), jnp.sum(norm_grad, axis=0)), "ctx"
    )
    ln_grads = jnp.stack([gain_sum, bias_sum]) * grad_scale
    owners = owner_map[0]
    image_count = owners.shape[0]
    image_rows = row_count // image_count
    capacity = max(1, 2 * image_count // tp_count)
    slot_of = slot_numbers(owners, capacity)
    slot_ids = jnp.arange(tp_count * capacity)
    matches = slot_of[None, :] == slot_ids[:, None]
    present = jnp.any(matches, axis=1)
    source_image = jnp.sum(jnp.where(matches, jnp.arange(image_count)[None, :], 0), axis=1)
    images = visual.reshape(image_count, image_rows, visual.shape[1])
    picked = jnp.take(images, source_image, axis=0)
    outgoing = jnp.where(present[:, None, None], picked, jnp.zeros((), jnp.bfloat16)).reshape(
        tp_count * capacity * image_rows, visual.shape[1]
    )
    vit_grad = lax.all_to_all(outgoing, "tp", split_axis=0, concat_axis=1, tiled=True)
    return (grad_w2, grad_w1, bias_up * grad_scale, bias_down * grad_scale, ln_grads, vit_grad)


def solution(mesh):
    return jax.shard_map(
        per_device,
        mesh=mesh,
        in_specs=(
            P("ctx", "tp"),
            P("ctx", "tp"),
            P("ctx", "tp"),
            P("ctx"),
            P(None, "tp"),
            P(None, "tp"),
            P("tp"),
            P("ctx", None),
        ),
        out_specs=(
            P("ctx", "tp"),
            P("ctx", "tp"),
            P("tp"),
            P("tp"),
            P(None, "tp"),
            P(("ctx", "tp"), None),
        ),
        check_vma=False,
    )
```

profile of v0, /device:TPU:6, one launch (start us, length us, event | category | flops | bytes accessed | tf_op | source)
XLA Modules:
  0.0 356.5 jit_solution(15268767459479100883)
XLA Ops:
  7.2 0.0 copy-start
  7.2 0.0 all-gather.3.cloned.1.call-start
  7.2 0.7 all-gather.3.cloned.1.call-update
  7.9 0.0 copy-start.4
  7.9 0.0 all-gather.5.cloned.1.call-start
  8.0 83.0 %all-gather.3.cloned.1.call-done = bf16[1024,4096]{1,0:T(8,128)(2,1)} async-done(((bf16[1024,256]{1,0:T(8,128)(2,1)}), bf16[1024,4096]{1,0:T(8,128)(2,1)}) %all-gather.3.cloned.1.call-update) | async-done | bytes 8388624 | tf_op jit(solution)/shard_map/all_gather | solution.py:33
  91.0 0.0 copy-done
  91.0 6.8 %convert_reduce_fusion.1 = (f32[256]{0:T(256)S(1)}, bf16[1024,256]{1,0:T(8,128)(2,1)}) fusion(bf16[1024,256]{1,0:T(8,128)(2,1)} %param.9, bf16[1024,4096]{1,0:T(8,128)(2,1)} %all-gather.3.cloned.1.call-done, bf16[4096,256]{1,0:T(8,128)(2,1)S(1)} %copy-done), kind=kOutput, calls=%fused_computation.28 | convolution fusion | flops 2150891264 | bytes 11535360 | tf_op jit(solution)/shard_map/dot_general | solution.py:34
  97.8 0.0 all-gather.5.cloned.1.call-update
  97.8 0.0 reduce-scatter.3.cloned.1.call-start
  97.8 0.0 copy-done.4
  97.9 7.8 %convolution_bitcast_fusion = f32[4096,256]{0,1:T(8,128)} fusion(bf16[1024,4096]{1,0:T(8,128)(2,1)} %all-gather.3.cloned.1.call-done, bf16[1024,256]{1,0:T(8,128)(2,1)S(1)} %copy-done.4), kind=kOutput, calls=%fused_computation.2 | convolution fusion | flops 2149056512 | bytes 13107200 | tf_op jit(solution)/shard_map/dot_general | solution.py:21
  105.7 0.0 copy-start.3
  105.7 0.0 reduce-scatter.3.cloned.1.call-update
  105.7 0.0 reduce-scatter.5.cloned.1.call-start
  105.8 69.9 %all-gather.5.cloned.1.call-done = bf16[1024,4096]{1,0:T(8,128)(2,1)} async-done(((bf16[1024,256]{1,0:T(8,128)(2,1)}), bf16[1024,4096]{1,0:T(8,128)(2,1)}) %all-gather.5.cloned.1.call-update) | async-done | bytes 8388624 | tf_op jit(solution)/shard_map/all_gather | solution.py:48
  175.7 0.0 copy-done.3
  175.7 13.2 %fusion.19 = f32[4096,800]{0,1:T(8,128)} fusion(bf16[1024,800]{0,1:T(8,128)(2,1)S(1)} %copy-done.3, bf16[1024,4096]{1,0:T(8,128)(2,1)} %all-gather.5.cloned.1.call-done), kind=kOutput, calls=%fused_computation.49 | convolution fusion | flops 6710886400 | bytes 23134208 | tf_op jit(solution)/shard_map/dot_general | solution.py:21
  188.9 0.0 copy-start.7
  188.9 0.0 copy-start.5
  188.9 0.0 reduce-scatter.5.cloned.1.call-update
  188.9 0.6 copy-done.7
  189.5 0.2 convert_reduce_fusion.2
  189.7 0.1 select_reduce_fusion
  189.8 0.1 fusion.14
  189.9 0.0 copy-done.5
  189.9 0.0 copy-start.6
  190.0 13.3 %fusion.1 = (f32[1024]{0:T(1024)S(1)}, f32[800]{0:T(1024)S(1)}, f32[1024]{0:T(1024)S(1)}, f32[800]{0:T(1024)S(1)}, f32[1024,800]{0,1:T(8,128)}) fusion(bf16[1024,800]{0,1:T(8,128)(2,1)S(1)} %copy-done.3, f32[800]{0:T(1024)S(1)} %copy-done.5, bf16[1024,4096]{1,0:T(8,128)(2,1)} %all-gather.5.cloned.1.call-done, bf16[4096,800]{0,1:T(8,128)(2,1)} %param.12), kind=kOutput, calls=%fused_computation.7 | convolution fusion | flops 6717435904 | bytes 19875200 | tf_op jit(solution)/shard_map/dot_general | solution.py:54
  203.2 38.8 %all-reduce = (f32[1024]{0:T(1024)S(1)}, f32[1024]{0:T(1024)S(1)}) all-reduce(f32[1024]{0:T(1024)S(1)} %get-tuple-element.24, f32[1024]{0:T(1024)S(1)} %get-tuple-element.26), channel_id=1, replica_groups=mesh['ctx'=8,'tp'=16] {'tp'}, use_global_device_ids=true, to_apply=%region_16.17 | all-reduce | flops 2048 | bytes 16384 | tf_op jit(solution)/shard_map/psum | solution.py:57
  242.1 0.0 copy-done.6
  242.1 2.7 fusion.4
  244.8 0.1 copy.24
  244.9 3.8 %gather_fusion = bf16[16,256,800]{1,2,0:T(8,128)(2,1)} fusion(bf16[4,256,800]{1,2,0:T(8,128)(2,1)S(1)} %bitcast.27, s32[1024]{0:T(1024)S(1)} %pad_clamp_fusion), kind=kCustom, calls=%fused_computation | custom fusion | bytes 13107264 | tf_op jit(solution)/shard_map/jit(_take)/gather | solution.py:80
  248.7 6.6 %select_select_fusion = bf16[16,256,800]{1,2,0:T(8,128)(2,1)} fusion(bf16[16,256,800]{1,2,0:T(8,128)(2,1)} %gather_fusion, pred[16]{0:T(512)(128)(4,1)S(1)} %compare_and_fusion, pred[16]{0:T(512)(128)(4,1)S(1)} %fusion.14), kind=kLoop, calls=%fused_computation.1 | loop fusion | flops 6553600 | bytes 13107232 | tf_op jit(solution)/shard_map/jit(_where)/select_n | solution.py:81
  255.2 0.0 copy-start.2
  255.2 4.8 %all-to-all-start = ((bf16[16,256,800]{1,2,0:T(8,128)(2,1)}), bf16[16,256,800]{1,2,0:T(8,128)(2,1)}, u32[]{:S(2)}, u32[]{:S(2)}) async-start(bf16[16,256,800]{1,2,0:T(8,128)(2,1)} %select_select_fusion), calls=%async_computation.2 | async-start | bytes 13107200 | tf_op jit(solution)/shard_map/all_to_all | solution.py:84
  260.1 0.0 copy-done.2
  260.1 0.2 convert_reduce_fusion
  260.2 0.0 reduce-scatter.3.cloned.1.call-done
  260.3 1.1 broadcast_multiply_fusion.1
  261.4 1.0 copy.20
  262.4 12.1 %all-reduce.1 = (f32[256]{0:T(256)S(1)}, f32[256]{0:T(256)S(1)}, f32[1,800]{1,0:T(1,128)S(1)}, f32[1,800]{1,0:T(1,128)S(1)}) all-reduce(f32[256]{0:T(256)S(1)} %get-tuple-element.34, f32[256]{0:T(256)S(1)} %convert_reduce_fusion, f32[1,800]{1,0:T(1,128)S(1)} %stack.10, f32[1,800]{1,0:T(1,128)S(1)} %stack.9), channel_id=1, replica_groups=mesh['ctx'=8,'tp'=16] {'ctx'}, use_global_device_ids=true, to_apply=%region_3.0 | all-reduce | flops 2112 | bytes 16896 | tf_op jit(solution)/shard_map/psum | solution.py:41
  274.5 0.6 maximum_multiply_fusion
  275.1 0.6 broadcast_multiply_fusion.4
  275.7 61.9 %all-to-all-done = bf16[16,256,800]{1,2,0:T(8,128)(2,1)} async-done(((bf16[16,256,800]{1,2,0:T(8,128)(2,1)}), bf16[16,256,800]{1,2,0:T(8,128)(2,1)}, u32[]{:S(2)}, u32[]{:S(2)}) %all-to-all-start) | async-done | bytes 6553632 | tf_op jit(solution)/shard_map/all_to_all | solution.py:84
  337.5 9.7 %copy.21 = bf16[256,12800]{1,0:T(8,128)(2,1)} copy(bf16[256,12800]{0,1:T(8,128)(2,1)} %bitcast.7) | data formatting | bytes 13107200
  347.2 2.8 broadcast_multiply_fusion
  350.0 0.0 copy-done.1
  (9 shorter events, 0.0 us)
Async XLA Ops:
  7.2 83.8 %copy-start = (bf16[4096,256]{1,0:T(8,128)(2,1)S(1)}, bf16[4096,256]{1,0:T(8,128)(2,1)}, u32[]{:S(2)}) copy-start(bf16[4096,256]{1,0:T(8,128)(2,1)} %param.13) | copy-start | bytes 6291460
  7.2 83.8 %all-gather.3.cloned.1.call-start = ((), (), s32[]{:S(2)}) async-start(), calls=%async_computation.3 | async-start | bytes 8912896 | tf_op jit(solution)/shard_map/all_gather | solution.py:33
  7.9 89.9 %copy-start.4 = (bf16[1024,256]{1,0:T(8,128)(2,1)S(1)}, bf16[1024,256]{1,0:T(8,128)(2,1)}, u32[]{:S(2)}) copy-start(bf16[1024,256]{1,0:T(8,128)(2,1)} %param.9) | copy-start | bytes 1572868
  7.9 167.8 %all-gather.5.cloned.1.call-start = ((), (), s32[]{:S(2)}) async-start(), calls=%async_computation.5 | async-start | bytes 8912896 | tf_op jit(solution)/shard_map/all_gather | solution.py:48
  97.8 162.5 %reduce-scatter.3.cloned.1.call-start = ((), (), s32[]{:S(2)}) async-start(), calls=%async_computation.4 | async-start | bytes 4718592 | tf_op jit(solution)/shard_map/reduce_scatter | solution.py:38
  105.7 70.0 %copy-start.3 = (bf16[1024,800]{0,1:T(8,128)(2,1)S(1)}, bf16[1024,800]{0,1:T(8,128)(2,1)}, u32[]{:S(2)}) copy-start(bf16[1024,800]{0,1:T(8,128)(2,1)} %param.10) | copy-start | bytes 4915204
  105.7 241.5 %reduce-scatter.5.cloned.1.call-start = ((), (), s32[]{:S(2)}) async-start(), calls=%async_computation.6 | async-start | bytes 14745600 | tf_op jit(solution)/shard_map/reduce_scatter | solution.py:51
  188.9 0.7 copy-start.7
  188.9 1.0 copy-start.5
  189.9 52.2 %copy-start.6 = (f32[1024]{0:T(1024)S(1)}, f32[1024]{0:T(1024)}, u32[]{:S(2)}) copy-start(f32[1024]{0:T(1024)} %param.11) | copy-start | bytes 12292
  255.2 4.8 %copy-start.2 = (bf16[1024,256]{1,0:T(8,128)(2,1)S(1)}, bf16[1024,256]{1,0:T(8,128)(2,1)}, u32[]{:S(2)}) copy-start(bf16[1024,256]{1,0:T(8,128)(2,1)} %param.8) | copy-start | bytes 1572868
  255.2 82.3 %all-to-all-start = ((bf16[16,256,800]{1,2,0:T(8,128)(2,1)}), bf16[16,256,800]{1,2,0:T(8,128)(2,1)}, u32[]{:S(2)}, u32[]{:S(2)}) async-start(bf16[16,256,800]{1,2,0:T(8,128)(2,1)} %select_select_fusion), calls=%async_computation.2 | async-start | bytes 13107200 | tf_op jit(solution)/shard_map/all_to_all | solution.py:84
  337.5 12.5 %copy-start.1 = (bf16[4096,256]{1,0:T(8,128)(2,1)S(1)}, bf16[4096,256]{1,0:T(8,128)(2,1)}, u32[]{:S(2)}) copy-start(bf16[4096,256]{1,0:T(8,128)(2,1)} %param.13) | copy-start | bytes 6291460
Sparse Core Ops, SparseCore 0:
  10.1 80.8 all-gather.2
  97.9 77.7 all-gather.4
  178.1 33.4 reduce-scatter.2
  213.9 76.0 reduce-scatter.4
where the time goes:
time: 357 us
  waiting for transfers between devices  216 us (61%)
  blocking collectives  51 us (14%)
  matrix products  41.1 us (12%)
  local copies, waits for them, and re-layouts  15.2 us (4%)
  other arithmetic  14.9 us (4%)
  between operations  13.9 us (4%)
  starting transfers between devices  4.98 us (1%)
    all_gather x1, waiting for transfers between devices, per_device(): full_grad = lax.all_gather(out_grad, 'tp', axis=1, tiled=True)  83 us
    all_gather x1, waiting for transfers between devices, per_device(): back_linear = lax.all_gather(back_part, 'tp', axis=1, tiled=True)  69.9 us
    all_to_all x1, waiting for transfers between devices, per_device(): lax.all_to_all(outgoing, 'tp', split_axis=0, concat_axis=1, tiled=True)  61.9 us
    psum x1, blocking collectives, per_device(): lax.psum((jnp.sum(gained, axis=-1), jnp.sum(gained * features, axis=-1)),...  38.8 us
    dot_general x2, matrix products, row_product(): lax.dot_general(left, right, (((0,), (0,)), ((), ())), preferred_element_...  21 us
    dot_general x1, matrix products, per_device(): norm_grad = jnp.dot(back_linear, w_up, preferred_element_type=jnp.float32)  13.3 us
    psum x1, blocking collectives, per_device(): lax.psum((jnp.sum(out_grad.astype(jnp.float32), axis=0), jnp.sum(back_par...  12.1 us
    unnamed x18, local copies, waits for them, and re-layouts  11.3 us
  transfers between devices with their start and end apart: 5, of which 3 were waited for; matrix products, arithmetic and copies ran while one was open for 17% of the time, Pallas kernels for 0%

commit v1 on v0

--- a/solution.py
+++ b/solution.py
@@ -45,7 +45,9 @@
         ),
         "ctx",
     )
-    back_linear = lax.all_gather(back_part, "tp", axis=1, tiled=True)
+    back_linear = jnp.concatenate(
+        lax.all_to_all(jnp.stack([back_part] * lax.axis_size("tp")), "tp", 0, 0), axis=1
+    )
     columns = back_linear
     grad_w1 = (
         lax.psum_scatter(row_product(columns, normed), "ctx", scatter_dimension=0, tiled=True)

time: 357 us -> 408 us (1.14)
  waiting for transfers between devices: 216 us -> 259 us
  starting transfers between devices: 4.98 us -> 10.1 us
  local copies, waits for them, and re-layouts: 15.2 us -> 19.7 us
    all_to_all x0 -> x1, waiting for transfers between devices: none -> 114 us  [per_device(): lax.all_to_all(jnp.stack([back_part] * lax.axis_size('tp')), 'tp', 0, 0)]
    all_gather x1 -> x0, waiting for transfers between devices: 69.9 us -> none  [per_device(): back_linear = lax.all_gather(back_part, 'tp', axis=1, tiled=True)]
    all_to_all x0 -> x1, starting transfers between devices: none -> 5.12 us  [per_device(): lax.all_to_all(jnp.stack([back_part] * lax.axis_size('tp')), 'tp', 0, 0)]
    another operation x0 -> x1, local copies, waits for them, and re-layouts: none -> 4.3 us  [per_device(): jnp.stack([back_part] * lax.axis_size('tp'))]
  transfers between devices with their start and end apart: 5 -> 5, of which waited for: 3 -> 3; matrix products, arithmetic and copies ran while one was open for 17% -> 15% of each run, Pallas kernels for 0% -> 0%
where the time goes in v1:
time: 408 us; the launch traced here: 407 us
  waiting for transfers between devices  259 us (63%)
  blocking collectives  49.4 us (12%)
  matrix products  40.1 us (10%)
  local copies, waits for them, and re-layouts  19.7 us (5%)
  other arithmetic  15 us (4%)
  between operations  13.9 us (3%)
  starting transfers between devices  10.1 us (2%)
    all_to_all x1, waiting for transfers between devices, per_device(): lax.all_to_all(jnp.stack([back_part] * lax.axis_size('tp')), 'tp', 0, 0)  114 us
    all_gather x1, waiting for transfers between devices, per_device(): full_grad = lax.all_gather(out_grad, 'tp', axis=1, tiled=True)  83.1 us
    all_to_all x1, waiting for transfers between devices, per_device(): lax.all_to_all(outgoing, 'tp', split_axis=0, concat_axis=1, tiled=True)  61.1 us
    psum x1, blocking collectives, per_device(): lax.psum((jnp.sum(gained, axis=-1), jnp.sum(gained * features, axis=-1)),...  38.6 us
    dot_general x2, matrix products, row_product(): lax.dot_general(left, right, (((0,), (0,)), ((), ())), preferred_element_...  21 us
    dot_general x1, matrix products, per_device(): norm_grad = jnp.dot(back_linear, w_up, preferred_element_type=jnp.float32)  13 us
    unnamed x18, local copies, waits for them, and re-layouts  11.3 us
    psum x1, blocking collectives, per_device(): lax.psum((jnp.sum(out_grad.astype(jnp.float32), axis=0), jnp.sum(back_par...  10.9 us
  transfers between devices with their start and end apart: 5, of which 3 were waited for; matrix products, arithmetic and copies ran while one was open for 15% of the time, Pallas kernels for 0%

profile of v1, /device:TPU:6, one launch (start us, length us, event | category | flops | bytes accessed | tf_op | source)
XLA Modules:
  0.0 407.4 jit_solution(8701531166109159338)
XLA Ops:
  7.2 0.0 copy-start
  7.2 0.0 all-gather.2.cloned.1.call-start
  7.2 0.7 all-gather.2.cloned.1.call-update
  7.9 83.1 %all-gather.2.cloned.1.call-done = bf16[1024,4096]{1,0:T(8,128)(2,1)} async-done(((bf16[1024,256]{1,0:T(8,128)(2,1)}), bf16[1024,4096]{1,0:T(8,128)(2,1)}) %all-gather.2.cloned.1.call-update) | async-done | bytes 8388624 | tf_op jit(solution)/shard_map/all_gather | solution.py:33
  91.0 0.0 copy-done
  91.0 6.0 %convert_reduce_fusion.1 = (f32[256]{0:T(256)S(1)}, bf16[1024,256]{1,0:T(8,128)(2,1)S(1)}) fusion(bf16[1024,256]{1,0:T(8,128)(2,1)} %param.9, bf16[1024,4096]{1,0:T(8,128)(2,1)} %all-gather.2.cloned.1.call-done, bf16[4096,256]{1,0:T(8,128)(2,1)S(1)} %copy-done), kind=kOutput, calls=%fused_computation.28 | convolution fusion | flops 2150891264 | bytes 11535360 | tf_op jit(solution)/shard_map/dot_general | solution.py:34
  97.0 0.2 copy.20
  97.2 4.3 %stack.8 = bf16[16,1024,256]{1,2,0:T(8,128)(2,1)} broadcast(bf16[1024,256]{0,1:T(8,128)(2,1)S(1)} %copy.20), dimensions={1,2} | broadcast | bytes 8912896 | tf_op jit(solution)/shard_map/stack | solution.py:49
  101.5 0.0 copy-start.4
  101.5 5.1 %all-to-all-start = ((bf16[16,1024,256]{1,2,0:T(8,128)(2,1)}), bf16[16,1024,256]{1,2,0:T(8,128)(2,1)}, u32[]{:S(2)}, u32[]{:S(2)}) async-start(bf16[16,1024,256]{1,2,0:T(8,128)(2,1)} %stack.8), calls=%async_computation.1 | async-start | bytes 16777216 | tf_op jit(solution)/shard_map/all_to_all | solution.py:49
  106.6 0.0 reduce-scatter.3.cloned.1.call-start
  106.7 0.0 copy-done.4
  106.7 7.8 %convolution_bitcast_fusion = f32[4096,256]{0,1:T(8,128)} fusion(bf16[1024,4096]{1,0:T(8,128)(2,1)} %all-gather.2.cloned.1.call-done, bf16[1024,256]{1,0:T(8,128)(2,1)S(1)} %copy-done.4), kind=kOutput, calls=%fused_computation.2 | convolution fusion | flops 2149056512 | bytes 13107200 | tf_op jit(solution)/shard_map/dot_general | solution.py:21
  114.5 0.0 copy-start.3
  114.5 0.0 reduce-scatter.3.cloned.1.call-update
  114.5 0.0 reduce-scatter.5.cloned.1.call-start
  114.6 114.3 %all-to-all-done = bf16[16,1024,256]{1,2,0:T(8,128)(2,1)} async-done(((bf16[16,1024,256]{1,2,0:T(8,128)(2,1)}), bf16[16,1024,256]{1,2,0:T(8,128)(2,1)}, u32[]{:S(2)}, u32[]{:S(2)}) %all-to-all-start) | async-done | bytes 8388640 | tf_op jit(solution)/shard_map/all_to_all | solution.py:49
  228.8 0.0 copy-done.3
  228.8 13.3 %fusion.19 = f32[4096,800]{0,1:T(8,128)} fusion(bf16[1024,4096]{0,1:T(8,128)(2,1)} %bitcast.2, bf16[1024,800]{0,1:T(8,128)(2,1)S(1)} %copy-done.3), kind=kOutput, calls=%fused_computation.49 | convolution fusion | flops 6710886400 | bytes 23134208 | tf_op jit(solution)/shard_map/dot_general | solution.py:21
  242.1 0.0 copy-start.7
  242.1 0.0 copy-start.5
  242.1 0.0 reduce-scatter.5.cloned.1.call-update
  242.1 0.6 copy-done.7
  242.7 0.2 convert_reduce_fusion.2
  242.9 0.1 select_reduce_fusion
  243.0 0.1 fusion.14
  243.1 0.0 copy-done.5
  243.1 0.0 copy-start.6
  243.1 13.0 %fusion.1 = (f32[1024]{0:T(1024)S(1)}, f32[800]{0:T(1024)S(1)}, f32[1024]{0:T(1024)S(1)}, f32[800]{0:T(1024)S(1)}, f32[1024,800]{0,1:T(8,128)}) fusion(bf16[1024,800]{0,1:T(8,128)(2,1)S(1)} %copy-done.3, f32[800]{0:T(1024)S(1)} %copy-done.5, bf16[4096,800]{0,1:T(8,128)(2,1)} %param.12, bf16[1024,4096]{0,1:T(8,128)(2,1)} %bitcast.2), kind=kOutput, calls=%fused_computation.7 | convolution fusion | flops 6717435904 | bytes 19875200 | tf_op jit(solution)/shard_map/dot_general | solution.py:56
  256.2 38.6 %all-reduce = (f32[1024]{0:T(1024)S(1)}, f32[1024]{0:T(1024)S(1)}) all-reduce(f32[1024]{0:T(1024)S(1)} %get-tuple-element.24, f32[1024]{0:T(1024)S(1)} %get-tuple-element.26), channel_id=1, replica_groups=mesh['ctx'=8,'tp'=16] {'tp'}, use_global_device_ids=true, to_apply=%region_16.17 | all-reduce | flops 2048 | bytes 16384 | tf_op jit(solution)/shard_map/psum | solution.py:59
  294.8 0.0 copy-done.6
  294.8 2.8 fusion.4
  297.6 0.1 copy.26
  297.7 3.8 gather_fusion
  301.4 6.6 %select_select_fusion = bf16[16,256,800]{1,2,0:T(8,128)(2,1)} fusion(bf16[16,256,800]{1,2,0:T(8,128)(2,1)} %gather_fusion, pred[16]{0:T(512)(128)(4,1)S(1)} %compare_and_fusion, pred[16]{0:T(512)(128)(4,1)S(1)} %fusion.14), kind=kLoop, calls=%fused_computation.1 | loop fusion | flops 6553600 | bytes 13107232 | tf_op jit(solution)/shard_map/jit(_where)/select_n | solution.py:83
  308.0 0.0 copy-start.2
  308.0 4.8 %all-to-all-start.1 = ((bf16[16,256,800]{1,2,0:T(8,128)(2,1)}), bf16[16,256,800]{1,2,0:T(8,128)(2,1)}, u32[]{:S(2)}, u32[]{:S(2)}) async-start(bf16[16,256,800]{1,2,0:T(8,128)(2,1)} %select_select_fusion), calls=%async_computation.3 | async-start | bytes 13107200 | tf_op jit(solution)/shard_map/all_to_all | solution.py:86
  312.9 0.0 copy-done.2
  312.9 0.2 convert_reduce_fusion
  313.1 10.9 %all-reduce.1 = (f32[256]{0:T(256)S(1)}, f32[256]{0:T(256)S(1)}, f32[1,800]{1,0:T(1,128)S(1)}, f32[1,800]{1,0:T(1,128)S(1)}) all-reduce(f32[256]{0:T(256)S(1)} %get-tuple-element.34, f32[256]{0:T(256)S(1)} %convert_reduce_fusion, f32[1,800]{1,0:T(1,128)S(1)} %stack.10, f32[1,800]{1,0:T(1,128)S(1)} %stack.9), channel_id=1, replica_groups=mesh['ctx'=8,'tp'=16] {'ctx'}, use_global_device_ids=true, to_apply=%region_3.0 | all-reduce | flops 2112 | bytes 16896 | tf_op jit(solution)/shard_map/psum | solution.py:41
  323.9 0.6 maximum_multiply_fusion
  324.6 0.6 broadcast_multiply_fusion.4
  325.1 1.1 broadcast_multiply_fusion.1
  326.2 1.0 copy.22
  327.2 61.1 %all-to-all-done.1 = bf16[16,256,800]{1,2,0:T(8,128)(2,1)} async-done(((bf16[16,256,800]{1,2,0:T(8,128)(2,1)}), bf16[16,256,800]{1,2,0:T(8,128)(2,1)}, u32[]{:S(2)}, u32[]{:S(2)}) %all-to-all-start.1) | async-done | bytes 6553632 | tf_op jit(solution)/shard_map/all_to_all | solution.py:86
  388.4 9.7 %copy.23 = bf16[256,12800]{1,0:T(8,128)(2,1)} copy(bf16[256,12800]{0,1:T(8,128)(2,1)} %bitcast.10) | data formatting | bytes 13107200
  398.1 2.8 broadcast_multiply_fusion
  400.8 0.0 copy-done.1
  (10 shorter events, 0.0 us)
Async XLA Ops:
  7.2 83.8 %copy-start = (bf16[4096,256]{1,0:T(8,128)(2,1)S(1)}, bf16[4096,256]{1,0:T(8,128)(2,1)}, u32[]{:S(2)}) copy-start(bf16[4096,256]{1,0:T(8,128)(2,1)} %param.13) | copy-start | bytes 6291460
  7.2 83.8 %all-gather.2.cloned.1.call-start = ((), (), s32[]{:S(2)}) async-start(), calls=%async_computation.4 | async-start | bytes 8912896 | tf_op jit(solution)/shard_map/all_gather | solution.py:33
  101.5 5.2 %copy-start.4 = (bf16[1024,256]{1,0:T(8,128)(2,1)S(1)}, bf16[1024,256]{1,0:T(8,128)(2,1)}, u32[]{:S(2)}) copy-start(bf16[1024,256]{1,0:T(8,128)(2,1)} %param.9) | copy-start | bytes 1572868
  101.5 127.3 %all-to-all-start = ((bf16[16,1024,256]{1,2,0:T(8,128)(2,1)}), bf16[16,1024,256]{1,2,0:T(8,128)(2,1)}, u32[]{:S(2)}, u32[]{:S(2)}) async-start(bf16[16,1024,256]{1,2,0:T(8,128)(2,1)} %stack.8), calls=%async_computation.1 | async-start | bytes 16777216 | tf_op jit(solution)/shard_map/all_to_all | solution.py:49
  106.6 218.5 %reduce-scatter.3.cloned.1.call-start = ((), (), s32[]{:S(2)}) async-start(), calls=%async_computation.5 | async-start | bytes 4718592 | tf_op jit(solution)/shard_map/reduce_scatter | solution.py:38
  114.5 114.3 %copy-start.3 = (bf16[1024,800]{0,1:T(8,128)(2,1)S(1)}, bf16[1024,800]{0,1:T(8,128)(2,1)}, u32[]{:S(2)}) copy-start(bf16[1024,800]{0,1:T(8,128)(2,1)} %param.10) | copy-start | bytes 4915204
  114.5 283.5 %reduce-scatter.5.cloned.1.call-start = ((), (), s32[]{:S(2)}) async-start(), calls=%async_computation.6 | async-start | bytes 14745600 | tf_op jit(solution)/shard_map/reduce_scatter | solution.py:53
  242.1 0.7 copy-start.7
  242.1 1.0 copy-start.5
  243.1 51.6 %copy-start.6 = (f32[1024]{0:T(1024)S(1)}, f32[1024]{0:T(1024)}, u32[]{:S(2)}) copy-start(f32[1024]{0:T(1024)} %param.11) | copy-start | bytes 12292
  308.0 4.9 %copy-start.2 = (bf16[1024,256]{1,0:T(8,128)(2,1)S(1)}, bf16[1024,256]{1,0:T(8,128)(2,1)}, u32[]{:S(2)}) copy-start(bf16[1024,256]{1,0:T(8,128)(2,1)} %param.8) | copy-start | bytes 1572868
  308.0 80.3 %all-to-all-start.1 = ((bf16[16,256,800]{1,2,0:T(8,128)(2,1)}), bf16[16,256,800]{1,2,0:T(8,128)(2,1)}, u32[]{:S(2)}, u32[]{:S(2)}) async-start(bf16[16,256,800]{1,2,0:T(8,128)(2,1)} %select_select_fusion), calls=%async_computation.3 | async-start | bytes 13107200 | tf_op jit(solution)/shard_map/all_to_all | solution.py:86
  388.4 12.5 %copy-start.1 = (bf16[4096,256]{1,0:T(8,128)(2,1)S(1)}, bf16[4096,256]{1,0:T(8,128)(2,1)}, u32[]{:S(2)}) copy-start(bf16[4096,256]{1,0:T(8,128)(2,1)} %param.13) | copy-start | bytes 6291460
Sparse Core Ops, SparseCore 0:
  10.1 80.8 all-gather.1
  114.6 36.5 reduce-scatter.2
  242.2 72.8 reduce-scatter.4
